TPU v7x, 256 devices: a whole 4x4x8 slice. The times are simulated.
256 devices in a mesh: wide: 64 (over x, z, y_hi), narrow: 4 (over y_lo, core).
Axes of the slice: x: 4, y: 4 (y_hi: 2, y_lo: 2; y = y_hi * 2 + y_lo), z: 8, core: 2. Of those that a mesh axis runs over, the one named last changes fastest.
Arguments:
- latent: bfloat16 [64, 32, 48, 256], P('wide', 'narrow'), may hold values from -12 to 12
- conv_first: bfloat16 [6912, 256], P(None, 'wide'), may hold values from -0.078125 to 0.078125
- conv_second: bfloat16 [6912, 256], P(None, 'wide'), may hold values from -0.078125 to 0.078125
- embed_weight: bfloat16 [1024, 2240], P(None, 'wide'), may hold values from -0.1875 to 0.1875
- qkv_weight: bfloat16 [3, 2240, 2240], P(None, None, 'narrow'), may hold values from -0.125 to 0.125
Outputs:
- mixed: bfloat16 [24576, 2240], P('wide', 'narrow')
All inputs are finite; a program needn't handle non-finite values.
Results may differ from a plain program's by a relative error of at most 0.011.
Values may be sent and summed in bfloat16 or wider, within the bound.
No kernel may reach another device: no remote copies, remote signals or barrier semaphores. Data moves between devices by JAX's collectives and lax.ppermute only.
A program may use at most 128 MiB of HBM per device.

v0:
```python
import jax
import jax.numpy as jnp
from jax import lax
from jax.sharding import PartitionSpec as P

HEAD_DIM = 112


def shifted(x, axis, by):
    size = lax.axis_size(axis)
    pairs = [(i, i + by) for i in range(size) if 0 <= i + by < size]
    return lax.ppermute(x, axis, pairs)


def extended(block, sides, width):
    for axis, dim in sides:
        count = lax.axis_size(axis)
        forward = [(i, i + 1) for i in range(count - 1)]
        backward = [(target, source) for source, target in forward]
        low = lax.ppermute(
            lax.slice_in_dim(block, block.shape[dim] - width, None, axis=dim), axis, forward
        )
        high = lax.ppermute(lax.slice_in_dim(block, 0, width, axis=dim), axis, backward)
        block = jnp.concatenate([low, block, high], axis=dim)
    return block


def laid_out(blocks, dim):
    lengths = list(blocks.shape[1:])
    lengths[dim] *= blocks.shape[0]
    return jnp.moveaxis(blocks, 0, dim).reshape(lengths)


def work_in_pieces(x, axis, dim, work, out_dim):
    extent = x.shape[dim]
    pieces = jnp.split(x, 2, axis=dim) if extent % 2 == 0 else [x]
    first = jnp.arange(lax.axis_size(axis)) * extent
    blocks = [lax.all_gather(share, axis) for share in pieces]
    made = [jax.vmap(work)(b, first + k * (extent // len(pieces))) for k, b in enumerate(blocks)]
    return laid_out(jnp.concatenate(made, axis=out_dim + 1), out_dim)


def exchange_in_groups(x, axis, split_dim, concat_dim, work, item_dim, out_dim):

    def moved(group):
        return lax.all_to_all(group, axis, split_axis=split_dim, concat_axis=concat_dim, tiled=True)

    items = jax.tree.leaves(x)[0].shape[item_dim]
    ends = [items * k // 2 for k in range(2 + 1)] if items % 2 == 0 else [0, items]
    groups = [
        jax.tree.map(lambda a: lax.slice_in_dim(a, low, high, axis=item_dim), x)
        for low, high in zip(ends, ends[1:])
    ]
    arrived = [moved(group) for group in groups]
    made = [work(group) for group in arrived]
    return jax.tree.map(lambda *parts: jnp.concatenate(parts, axis=out_dim), *made)


def causal_conv(current, weight):
    before = shifted(current, "wide", 1)
    earlier = shifted(current, "wide", 2)
    stacked = jnp.concatenate([earlier, before, current], axis=0)
    rimmed = extended(stacked, (("narrow", 1),), 1)
    padded = jnp.pad(rimmed, ((0, 0), (0, 0), (1, 1), (0, 0)))
    row_count = current.shape[1]
    col_count = current.shape[2]
    chan_count = current.shape[3]
    block_cols = lax.all_gather(weight, "wide", axis=1, tiled=True)
    summed = jnp.zeros((row_count * col_count, block_cols.shape[1]), jnp.float32)
    for kernel_tap in range(27):
        time_step = kernel_tap // 9
        row_step = kernel_tap // 3 % 3
        col_step = kernel_tap % 3
        window = padded[time_step, row_step : row_step + row_count, col_step : col_step + col_count]
        window = window.reshape(row_count * col_count, chan_count)
        summed = summed + jnp.dot(
            window,
            block_cols[kernel_tap * chan_count : (kernel_tap + 1) * chan_count],
            preferred_element_type=jnp.float32,
        )
    return summed


def embed_tokens(patch_feats, embed_weight):

    def project(block_cols, offset):
        return jnp.dot(patch_feats, block_cols, preferred_element_type=jnp.float32)

    return work_in_pieces(embed_weight, "wide", 1, project, 1).astype(jnp.bfloat16)


def per_device(latent, conv_first, conv_second, embed_weight, qkv_weight):
    row_count = latent.shape[1]
    col_count = latent.shape[2]
    chan_count = latent.shape[3]
    first = causal_conv(latent, conv_first)
    activated = jax.nn.silu(first).astype(jnp.bfloat16).reshape(latent.shape)
    second = causal_conv(activated, conv_second) + latent.reshape(-1, chan_count).astype(
        jnp.float32
    )
    block_out = second.astype(jnp.bfloat16)
    patches = block_out.reshape(row_count // 2, 2, col_count // 2, 2, chan_count)
    patches = patches.transpose(0, 2, 1, 3, 4).reshape(-1, 4 * chan_count)
    whole_patches = lax.all_gather(patches, "narrow", axis=0, tiled=True)
    embedded = embed_tokens(whole_patches, embed_weight)
    heads_here = qkv_weight.shape[2] // HEAD_DIM
    token_count = embedded.shape[0]
    query_raw = jnp.dot(embedded, qkv_weight[0], preferred_element_type=jnp.float32)
    key_raw = jnp.dot(embedded, qkv_weight[1], preferred_element_type=jnp.float32)
    val_rows = jnp.dot(embedded, qkv_weight[2], preferred_element_type=jnp.float32).astype(
        jnp.bfloat16
    )
    query_feat = (
        (jax.nn.elu(query_raw) + 1.0)
        .astype(jnp.bfloat16)
        .reshape(token_count, heads_here, HEAD_DIM)
    )
    key_feat = (
        (jax.nn.elu(key_raw) + 1.0).astype(jnp.bfloat16).reshape(token_count, heads_here, HEAD_DIM)
    )
    val_heads = val_rows.reshape(token_count, heads_here, HEAD_DIM)
    scores = jnp.einsum("thd,shd->hts", query_feat, key_feat, preferred_element_type=jnp.float32)
    row_ids = lax.broadcasted_iota(jnp.int32, (token_count, token_count), 0)
    col_ids = lax.broadcasted_iota(jnp.int32, (token_count, token_count), 1)
    scores = jnp.where((col_ids <= row_ids)[None], scores, 0.0)
    local_den = jnp.sum(scores, axis=-1)
    local_num = jnp.einsum(
        "hts,she->the", scores.astype(jnp.bfloat16), val_heads, preferred_element_type=jnp.float32
    )
    state_local = jnp.einsum(
        "thd,the->hde", key_feat, val_heads, preferred_element_type=jnp.float32
    )
    key_local = jnp.sum(key_feat, axis=0, dtype=jnp.float32)
    flat_state = jnp.concatenate([state_local.reshape(-1), key_local.reshape(-1)])
    length_all = flat_state.shape[0]
    peer_count = lax.axis_size("wide")
    per_peer = -(-length_all // peer_count)
    piece_grid = jnp.pad(flat_state, (0, per_peer * peer_count - length_all)).reshape(
        peer_count, per_peer
    )
    lower_ones = (
        lax.broadcasted_iota(jnp.int32, (peer_count, peer_count), 1)
        < lax.broadcasted_iota(jnp.int32, (peer_count, peer_count), 0)
    ).astype(jnp.float32)

    def running(columns_in):
        partial_sums = jnp.dot(lower_ones, columns_in, precision=lax.Precision.HIGHEST)
        return lax.all_to_all(
            partial_sums.astype(jnp.bfloat16), "wide", split_axis=0, concat_axis=0, tiled=True
        ).astype(partial_sums.dtype)

    spread = exchange_in_groups(
        piece_grid.astype(jnp.bfloat16),
        "wide",
        0,
        0,
        lambda group: running(group.astype(jnp.float32)),
        1,
        1,
    )
    flat_prefix = spread.reshape(-1)[:length_all]
    state_size = state_local.size
    state_prev = flat_prefix[:state_size].reshape(state_local.shape)
    key_prev = flat_prefix[state_size:].reshape(key_local.shape)
    query_wide = query_feat.astype(jnp.float32)
    carried_num = jnp.einsum(
        "thd,hde->the", query_wide, state_prev, precision=lax.Precision.HIGHEST
    )
    carried_den = jnp.einsum("thd,hd->th", query_wide, key_prev, precision=lax.Precision.HIGHEST)
    result = (local_num + carried_num) / (local_den.T + carried_den)[..., None]
    return result.astype(jnp.bfloat16).reshape(token_count, heads_here * HEAD_DIM)


def solution(mesh):
    return jax.shard_map(
        per_device,
        mesh=mesh,
        in_specs=(
            P("wide", "narrow", None, None),
            P(None, "wide"),
            P(None, "wide"),
            P(None, "wide"),
            P(None, None, "narrow"),
        ),
        out_specs=P("wide", "narrow"),
        check_vma=False,
    )
```

profile of v0, /device:TPU:8, one launch (start us, length us, event | category | flops | bytes accessed | tf_op | source)
XLA Modules:
  0.0 465.5 jit_solution(17870810909222242809)
XLA Ops:
  8.1 3.8 collective-permute-start
  11.9 4.2 collective-permute-start.1
  16.4 3.9 collective-permute-done.1
  20.3 1.0 constant_dynamic-update-slice_fusion
  21.4 1.9 collective-permute-start.2
  23.3 3.6 collective-permute-start.3
  27.0 1.9 collective-permute-done.3
  29.4 1.8 fusion.150
  31.2 1.1 pad_maximum_fusion.10
  32.3 105.1 %all-gather.9.cloned.1.call-done = bf16[64,4,6912]{2,1,0:T(4,128)(2,1)} async-done(((bf16[1,4,6912]{2,1,0:T(4,128)(2,1)}), bf16[64,4,6912]{2,1,0:T(4,128)(2,1)}) %all-gather.9.cloned.1.call-update) | async-done | bytes 3538960 | tf_op jit(solution)/shard_map/all_gather | solution.py:68
  137.5 5.3 %reshape.81 = bf16[256,6912]{1,0:T(8,128)(2,1)S(1)} reshape(bf16[64,4,6912]{2,1,0:T(4,128)(2,1)} %all-gather.9.cloned.1.call-done) | data formatting | bytes 7077888
  142.8 1.2 fusion.142
  144.1 1.2 fusion.136
  145.2 1.2 fusion.132
  146.4 1.2 fusion.128
  147.6 1.2 fusion.124
  154.7 2.8 collective-permute-start.4
  157.6 3.3 collective-permute-start.5
  160.9 3.1 collective-permute-done.5
  164.1 0.7 pad_maximum_fusion.18
  164.8 1.9 collective-permute-start.7
  167.4 94.9 %all-gather.11.cloned.1.call-done = bf16[64,4,6912]{2,1,0:T(4,128)(2,1)} async-done(((bf16[1,4,6912]{2,1,0:T(4,128)(2,1)}), bf16[64,4,6912]{2,1,0:T(4,128)(2,1)}) %all-gather.11.cloned.1.call-update) | async-done | bytes 3538960 | tf_op jit(solution)/shard_map/all_gather | solution.py:68
  262.3 5.3 %reshape.83 = bf16[256,6912]{1,0:T(8,128)(2,1)S(1)} reshape(bf16[64,4,6912]{2,1,0:T(4,128)(2,1)} %all-gather.11.cloned.1.call-done) | data formatting | bytes 7077888
  267.6 1.9 collective-permute-start.6
  269.6 1.2 pad_maximum_fusion
  270.8 2.7 collective-permute-done.6
  273.5 1.2 pad_maximum_fusion.3
  274.7 1.6 select_maximum_fusion
  283.4 0.9 fusion.41
  284.3 1.0 reshape.69
  285.6 7.4 %all_gather.17 = bf16[384,1024]{1,0:T(8,128)(2,1)S(1)} all-gather(bf16[96,1024]{1,0:T(8,128)(2,1)S(1)} %reshape.70), channel_id=1, replica_groups=mesh['wide'=64,'narrow'=4] {'narrow'}, dimensions={0}, use_global_device_ids=true | all-gather | bytes 983040 | tf_op jit(solution)/shard_map/all_gather | solution.py:104
  293.0 101.8 %all-gather.7.cloned.1.call-done = bf16[65536,35]{0,1:T(8,128)(2,1)} async-done(((bf16[1024,35]{0,1:T(8,128)(2,1)}), bf16[65536,35]{0,1:T(8,128)(2,1)}) %all-gather.7.cloned.1.call-update) | async-done | bytes 4587536 | tf_op jit(solution)/shard_map/all_gather | solution.py:38
  394.7 5.5 %copy.29 = bf16[5,8,64,1024]{3,2,1,0:T(8,128)(2,1)S(1)} copy(bf16[5,8,64,1024]{3,1,2,0:T(8,128)(2,1)} %bitcast.244) | data formatting | bytes 10485760
  400.2 2.6 fusion.12
  402.8 1.0 copy.19
  403.8 1.5 convert_element_type.63
  405.4 4.2 fusion.152
  409.6 3.2 fusion.22
  413.4 0.9 convert_element_type.72
  414.4 8.1 %all-to-all-start = ((bf16[64,1,989]{2,1,0:T(2,128)(2,1)}), bf16[64,1,989]{2,1,0:T(2,128)(2,1)S(1)}, u32[]{:S(2)}, u32[]{:S(2)}) async-start(bf16[64,1,989]{2,1,0:T(2,128)(2,1)} %convert_element_type.72), calls=%async_computation | async-start | bytes 524288 | tf_op jit(solution)/shard_map/all_to_all | solution.py:46
  422.5 3.5 fusion.49
  425.9 9.1 %all-to-all-done = bf16[64,1,989]{2,1,0:T(2,128)(2,1)S(1)} async-done(((bf16[64,1,989]{2,1,0:T(2,128)(2,1)}), bf16[64,1,989]{2,1,0:T(2,128)(2,1)S(1)}, u32[]{:S(2)}, u32[]{:S(2)}) %all-to-all-start) | async-done | bytes 126624 | tf_op jit(solution)/shard_map/all_to_all | solution.py:46
  435.2 0.9 copy.22
  436.1 5.8 %all-to-all-start.1 = ((bf16[64,1,989]{2,1,0:T(2,128)(2,1)}), bf16[64,1,989]{2,1,0:T(2,128)(2,1)S(1)}, u32[]{:S(2)}, u32[]{:S(2)}) async-start(bf16[64,1,989]{2,1,0:T(2,128)(2,1)} %copy.22), calls=%async_computation.1 | async-start | bytes 524288 | tf_op jit(solution)/shard_map/all_to_all | solution.py:148
  441.9 1.8 select_reduce_fusion
  443.8 10.7 %all-to-all-done.1 = bf16[64,1,989]{2,1,0:T(2,128)(2,1)S(1)} async-done(((bf16[64,1,989]{2,1,0:T(2,128)(2,1)}), bf16[64,1,989]{2,1,0:T(2,128)(2,1)S(1)}, u32[]{:S(2)}, u32[]{:S(2)}) %all-to-all-start.1) | async-done | bytes 126624 | tf_op jit(solution)/shard_map/all_to_all | solution.py:148
  454.5 0.8 reduce.2
  456.3 2.6 fusion.25
  (143 shorter events, 17.4 us)
Async XLA Ops:
  6.5 130.9 %all-gather.9.cloned.1.call-start = ((), (), s32[]{:S(2)}) async-start(), calls=%async_computation.3 | async-start | bytes 3594240 | tf_op jit(solution)/shard_map/all_gather | solution.py:68
  7.3 255.1 %all-gather.11.cloned.1.call-start = ((), (), s32[]{:S(2)}) async-start(), calls=%async_computation.4 | async-start | bytes 3594240 | tf_op jit(solution)/shard_map/all_gather | solution.py:68
  8.0 386.7 %all-gather.7.cloned.1.call-start = ((), (), s32[]{:S(2)}) async-start(), calls=%async_computation.2 | async-start | bytes 5324800 | tf_op jit(solution)/shard_map/all_gather | solution.py:38
  8.1 8.3 %collective-permute-start = (bf16[1,8,48,256]{3,2,1,0:T(8,128)(2,1)}, bf16[1,8,48,256]{3,2,1,0:T(8,128)(2,1)S(1)}, u32[]{:S(2)}, u32[]{:S(2)}) collective-permute-start(bf16[1,8,48,256]{3,2,1,0:T(8,128)(2,1)} %param.5), channel_id=1, source_target_pairs={{0,8},{4,12},{8,16},{12,20},{16,24},{20,28},{24,32},{28,36},{32,40... | collective-permute-start | bytes 589832 | tf_op jit(solution)/shard_map/ppermute | solution.py:12
  11.9 8.4 %collective-permute-start.1 = (bf16[1,8,48,256]{3,2,1,0:T(8,128)(2,1)}, bf16[1,8,48,256]{3,2,1,0:T(8,128)(2,1)S(1)}, u32[]{:S(2)}, u32[]{:S(2)}) collective-permute-start(bf16[1,8,48,256]{3,2,1,0:T(8,128)(2,1)} %param.5), channel_id=1, source_target_pairs={{0,4},{4,8},{8,12},{12,16},{16,20},{20,24},{24,28},{28,32},{32,36}... | collective-permute-start | bytes 589832 | tf_op jit(solution)/shard_map/ppermute | solution.py:12
  16.3 5.0 %copy-start.29 = (bf16[1,8,48,256]{3,2,1,0:T(8,128)(2,1)}, bf16[1,8,48,256]{3,2,1,0:T(8,128)(2,1)S(1)}, u32[]{:S(2)}) copy-start(bf16[1,8,48,256]{3,2,1,0:T(8,128)(2,1)S(1)} %collective-permute-done) | copy-start | bytes 589828
  20.3 1.0 copy-start.27
  21.4 5.7 %collective-permute-start.2 = (bf16[3,1,48,256]{3,2,1,0:T(8,128)(2,1)S(1)}, bf16[3,1,48,256]{3,2,1,0:T(8,128)(2,1)S(1)}, u32[]{:S(2)}, u32[]{:S(2)}) collective-permute-start(bf16[3,1,48,256]{3,2,1,0:T(8,128)(2,1)S(1)} %get-tuple-element.58), channel_id=1, source_target_pairs={{0,1},{1,2},{2,3},{4,5},{5,6},{6,7},{8,9},{9,10},{10,11},{12,13},{... | collective-permute-start | bytes 221192 | tf_op jit(solution)/shard_map/ppermute | solution.py:20
  23.3 5.7 %collective-permute-start.3 = (bf16[3,1,48,256]{3,2,1,0:T(8,128)(2,1)S(1)}, bf16[3,1,48,256]{3,2,1,0:T(8,128)(2,1)S(1)}, u32[]{:S(2)}, u32[]{:S(2)}) collective-permute-start(bf16[3,1,48,256]{3,2,1,0:T(8,128)(2,1)S(1)} %get-tuple-element.59), channel_id=1, source_target_pairs={{1,0},{2,1},{3,2},{5,4},{6,5},{7,6},{9,8},{10,9},{11,10},{13,12},{... | collective-permute-start | bytes 221192 | tf_op jit(solution)/shard_map/ppermute | solution.py:23
  142.8 6.1 %copy-start.11 = (bf16[1,8,48,256]{3,2,1,0:T(8,128)(2,1)S(1)}, bf16[1,8,48,256]{3,2,1,0:T(8,128)(2,1)}, u32[]{:S(2)}) copy-start(bf16[1,8,48,256]{3,2,1,0:T(8,128)(2,1)} %get-tuple-element.28) | copy-start | bytes 589828
  142.8 6.3 %copy-start.10 = (bf16[1,8,48,256]{3,2,1,0:T(8,128)(2,1)S(1)}, bf16[1,8,48,256]{3,2,1,0:T(8,128)(2,1)}, u32[]{:S(2)}) copy-start(bf16[1,8,48,256]{3,2,1,0:T(8,128)(2,1)} %get-tuple-element.26) | copy-start | bytes 589828
  142.8 6.6 %copy-start.26 = (bf16[1,8,48,256]{3,2,1,0:T(8,128)(2,1)S(1)}, bf16[1,8,48,256]{3,2,1,0:T(8,128)(2,1)}, u32[]{:S(2)}) copy-start(bf16[1,8,48,256]{3,2,1,0:T(8,128)(2,1)} %get-tuple-element.55) | copy-start | bytes 589828
  142.8 6.8 %copy-start.21 = (bf16[1,8,48,256]{3,2,1,0:T(8,128)(2,1)S(1)}, bf16[1,8,48,256]{3,2,1,0:T(8,128)(2,1)}, u32[]{:S(2)}) copy-start(bf16[1,8,48,256]{3,2,1,0:T(8,128)(2,1)} %get-tuple-element.38) | copy-start | bytes 589828
  142.8 7.1 %copy-start.20 = (bf16[1,8,48,256]{3,2,1,0:T(8,128)(2,1)S(1)}, bf16[1,8,48,256]{3,2,1,0:T(8,128)(2,1)}, u32[]{:S(2)}) copy-start(bf16[1,8,48,256]{3,2,1,0:T(8,128)(2,1)} %get-tuple-element.37) | copy-start | bytes 589828
  145.2 4.9 %copy-start.30 = (bf16[1,8,48,256]{3,2,1,0:T(8,128)(2,1)S(1)}, bf16[1,8,48,256]{3,2,1,0:T(8,128)(2,1)}, u32[]{:S(2)}) copy-start(bf16[1,8,48,256]{3,2,1,0:T(8,128)(2,1)} %copy-done.29) | copy-start | bytes 589828
  147.6 2.8 copy-start.19
  148.8 1.8 copy-start.25
  149.3 1.6 copy-start.18
  149.6 1.6 copy-start.24
  150.1 1.4 copy-start.17
  150.4 1.4 copy-start.28
  150.7 1.4 copy-start.16
  150.9 1.4 copy-start.23
  151.2 1.4 copy-start.15
  151.5 1.4 copy-start.22
  151.7 1.4 copy-start.14
  152.0 1.4 copy-start.6
  152.0 1.6 copy-start.13
  152.3 1.6 copy-start.9
  152.6 1.6 copy-start.12
  152.8 1.6 copy-start.31
  154.7 9.4 %copy-start = (bf16[384,256]{1,0:T(8,128)(2,1)}, bf16[384,256]{1,0:T(8,128)(2,1)S(1)}, u32[]{:S(2)}) copy-start(bf16[384,256]{1,0:T(8,128)(2,1)S(1)} %multiply_convert_fusion) | copy-start | bytes 589828
  154.7 6.2 %collective-permute-start.4 = (bf16[1,8,48,256]{3,2,1,0:T(8,128)(2,1)S(1)}, bf16[1,8,48,256]{3,2,1,0:T(8,128)(2,1)S(1)}, u32[]{:S(2)}, u32[]{:S(2)}) collective-permute-start(bf16[1,8,48,256]{3,2,1,0:T(8,128)(2,1)S(1)} %bitcast.246), channel_id=1, source_target_pairs={{0,8},{4,12},{8,16},{12,20},{16,24},{20,28},{24,32},{28,36},{32,40... | collective-permute-start | bytes 589832 | tf_op jit(solution)/shard_map/ppermute | solution.py:12
  157.6 6.5 %collective-permute-start.5 = (bf16[1,8,48,256]{3,2,1,0:T(8,128)(2,1)S(1)}, bf16[1,8,48,256]{3,2,1,0:T(8,128)(2,1)S(1)}, u32[]{:S(2)}, u32[]{:S(2)}) collective-permute-start(bf16[1,8,48,256]{3,2,1,0:T(8,128)(2,1)S(1)} %bitcast.247), channel_id=1, source_target_pairs={{0,4},{4,8},{8,12},{12,16},{16,20},{20,24},{24,28},{28,32},{32,36}... | collective-permute-start | bytes 589832 | tf_op jit(solution)/shard_map/ppermute | solution.py:12
  160.9 3.9 copy-start.4
  164.1 0.7 copy-start.2
  164.8 104.8 %collective-permute-start.7 = (bf16[3,1,48,256]{3,2,1,0:T(8,128)(2,1)}, bf16[3,1,48,256]{3,2,1,0:T(8,128)(2,1)}, u32[]{:S(2)}, u32[]{:S(2)}) collective-permute-start(bf16[3,1,48,256]{3,2,1,0:T(8,128)(2,1)} %get-tuple-element.54), channel_id=1, source_target_pairs={{1,0},{2,1},{3,2},{5,4},{6,5},{7,6},{9,8},{10,9},{11,10},{13,12},{... | collective-permute-start | bytes 221192 | tf_op jit(solution)/shard_map/ppermute | solution.py:23
  267.6 5.9 %collective-permute-start.6 = (bf16[3,1,48,256]{3,2,1,0:T(8,128)(2,1)}, bf16[3,1,48,256]{3,2,1,0:T(8,128)(2,1)S(1)}, u32[]{:S(2)}, u32[]{:S(2)}) collective-permute-start(bf16[3,1,48,256]{3,2,1,0:T(8,128)(2,1)} %get-tuple-element.53), channel_id=1, source_target_pairs={{0,1},{1,2},{2,3},{4,5},{5,6},{6,7},{8,9},{9,10},{10,11},{12,13},{... | collective-permute-start | bytes 221192 | tf_op jit(solution)/shard_map/ppermute | solution.py:20
  277.6 2.0 copy-start.5
  279.8 1.3 copy-start.3
  281.3 1.3 copy-start.1
  281.8 1.5 copy-start.7
  405.4 4.2 copy-start.8
  414.4 20.7 %all-to-all-start = ((bf16[64,1,989]{2,1,0:T(2,128)(2,1)}), bf16[64,1,989]{2,1,0:T(2,128)(2,1)S(1)}, u32[]{:S(2)}, u32[]{:S(2)}) async-start(bf16[64,1,989]{2,1,0:T(2,128)(2,1)} %convert_element_type.72), calls=%async_computation | async-start | bytes 524288 | tf_op jit(solution)/shard_map/all_to_all | solution.py:46
  422.5 19.5 %copy-start.32 = (pred[384,384]{0,1:T(8,128)(4,1)S(1)}, pred[384,384]{0,1:T(8,128)(4,1)}, u32[]{:S(2)}) copy-start(pred[384,384]{0,1:T(8,128)(4,1)} %iota_compare_fusion.2) | copy-start | bytes 442372
  436.1 18.3 %all-to-all-start.1 = ((bf16[64,1,989]{2,1,0:T(2,128)(2,1)}), bf16[64,1,989]{2,1,0:T(2,128)(2,1)S(1)}, u32[]{:S(2)}, u32[]{:S(2)}) async-start(bf16[64,1,989]{2,1,0:T(2,128)(2,1)} %copy.22), calls=%async_computation.1 | async-start | bytes 524288 | tf_op jit(solution)/shard_map/all_to_all | solution.py:148
Sparse Core Ops, SparseCore 0:
  10.8 126.5 all-gather.8
  140.9 121.3 all-gather.10
  265.9 128.8 all-gather.6
where the time goes:
time: 466 us; the launch traced here: 465 us
  waiting for transfers between devices  335 us (72%)
  starting transfers between devices  37.6 us (8%)
  matrix products  37.5 us (8%)
  local copies, waits for them, and re-layouts  26.1 us (6%)
  between operations  14.1 us (3%)
  other arithmetic  7.71 us (2%)
  blocking collectives  7.41 us (2%)
    all_gather x2, waiting for transfers between devices, causal_conv(): block_cols = lax.all_gather(weight, 'wide', axis=1, tiled=True)  200 us
    all_gather x1, waiting for transfers between devices, work_in_pieces(): blocks = [lax.all_gather(share, axis) for share in pieces]  102 us
    dot_general x54, matrix products, causal_conv(): jnp.dot(window, block_cols[kernel_tap * chan_count:(kernel_tap + 1) * cha...  18.6 us
    unnamed x71, local copies, waits for them, and re-layouts  16.3 us
    ppermute x4, starting transfers between devices, shifted(): return lax.ppermute(x, axis, pairs)  14.2 us
    all_to_all x1, waiting for transfers between devices, running(): lax.all_to_all(partial_sums.astype(jnp.bfloat16), 'wide', split_axis=0, c...  10.7 us
  transfers between devices with their start and end apart: 13, of which 11 were waited for; matrix products, arithmetic and copies ran while one was open for 10% of the time, Pallas kernels for 0%

commit v1 on v0

--- a/solution.py
+++ b/solution.py
@@ -1,9 +1,19 @@
+import functools
 import jax
 import jax.numpy as jnp
 from jax import lax
 from jax.sharding import PartitionSpec as P
 
 HEAD_DIM = 112
+
+
+def part_spot_by_axis(z, link_axis):
+    item_now = jnp.stack(tuple((z for _ in range(lax.axis_size(link_axis)))))
+    answer = lax.all_to_all(item_now, axis_name=link_axis, split_axis=0, concat_axis=0)
+    return jnp.concatenate(answer, 1)
+
+
+_mix_notes = functools.partial(part_spot_by_axis, link_axis="wide")
 
 
 def shifted(x, axis, by):
@@ -65,7 +75,7 @@
     row_count = current.shape[1]
     col_count = current.shape[2]
     chan_count = current.shape[3]
-    block_cols = lax.all_gather(weight, "wide", axis=1, tiled=True)
+    block_cols = _mix_notes(weight)
     summed = jnp.zeros((row_count * col_count, block_cols.shape[1]), jnp.float32)
     for kernel_tap in range(27):
         time_step = kernel_tap // 9

time: 466 us -> 365 us (0.78)
  waiting for transfers between devices: 335 us -> 126 us
  local copies, waits for them, and re-layouts: 26.1 us -> 87.2 us
  starting transfers between devices: 37.6 us -> 77.7 us
    all_gather x2 -> x0, waiting for transfers between devices: 200 us -> none  [causal_conv(): block_cols = lax.all_gather(weight, 'wide', axis=1, tiled=True)]
    all_gather x1, waiting for transfers between devices: 102 us -> 0.01 us  [work_in_pieces(): blocks = [lax.all_gather(share, axis) for share in pieces]]
    ppermute x4, waiting for transfers between devices: 7.29 us -> 75.2 us  [shifted(): return lax.ppermute(x, axis, pairs)]
    slice x0 -> x58, local copies, waits for them, and re-layouts: none -> 62.8 us  [causal_conv(): block_cols[kernel_tap * chan_count:(kernel_tap + 1) * chan_count]]
    all_to_all x0 -> x2, starting transfers between devices: none -> 31.1 us  [part_spot_by_axis(): lax.all_to_all(item_now, axis_name=link_axis, split_axis=0, concat_axis=0)]
    all_to_all x0 -> x2, waiting for transfers between devices: none -> 24.6 us  [part_spot_by_axis(): lax.all_to_all(item_now, axis_name=link_axis, split_axis=0, concat_axis=0)]
    unnamed x71 -> x141, local copies, waits for them, and re-layouts: 16.3 us -> 8.45 us
    another operation x0 -> x2, local copies, waits for them, and re-layouts: none -> 7.16 us  [part_spot_by_axis(): item_now = jnp.stack(tuple((z for _ in range(lax.axis_size(link_axis)))))]
  transfers between devices with their start and end apart: 13 -> 13, of which waited for: 11 -> 6; matrix products, arithmetic and copies ran while one was open for 10% -> 29% of each run, Pallas kernels for 0% -> 0%
where the time goes in v1:
time: 365 us; the launch traced here: 362 us
  waiting for transfers between devices  126 us (35%)
  local copies, waits for them, and re-layouts  87.2 us (24%)
  starting transfers between devices  77.7 us (21%)
  matrix products  40.6 us (11%)
  between operations  14.8 us (4%)
  other arithmetic  8.46 us (2%)
  blocking collectives  7.45 us (2%)
    ppermute x4, waiting for transfers between devices, shifted(): return lax.ppermute(x, axis, pairs)  75.2 us
    slice x58, local copies, waits for them, and re-layouts, causal_conv(): block_cols[kernel_tap * chan_count:(kernel_tap + 1) * chan_count]  62.8 us
    all_to_all x2, starting transfers between devices, part_spot_by_axis(): lax.all_to_all(item_now, axis_name=link_axis, split_axis=0, concat_axis=0)  31.1 us
    all_to_all x2, waiting for transfers between devices, part_spot_by_axis(): lax.all_to_all(item_now, axis_name=link_axis, split_axis=0, concat_axis=0)  24.6 us
    dot_general x54, matrix products, causal_conv(): jnp.dot(window, block_cols[kernel_tap * chan_count:(kernel_tap + 1) * cha...  21.8 us
    ppermute x4, starting transfers between devices, shifted(): return lax.ppermute(x, axis, pairs)  19.5 us
    all_to_all x1, waiting for transfers between devices, running(): lax.all_to_all(partial_sums.astype(jnp.bfloat16), 'wide', split_axis=0, c...  11.7 us
    all_to_all x1, waiting for transfers between devices, moved(): lax.all_to_all(group, axis, split_axis=split_dim, concat_axis=concat_dim,...  10.6 us
  transfers between devices with their start and end apart: 13, of which 6 were waited for; matrix products, arithmetic and copies ran while one was open for 29% of the time, Pallas kernels for 0%

profile of v1, /device:TPU:8, one launch (start us, length us, event | category | flops | bytes accessed | tf_op | source)
XLA Modules:
  0.0 362.2 jit_solution(9391280591101576367)
XLA Ops:
  6.5 3.6 stack.4
  10.1 13.7 %all-to-all-start = ((bf16[64,6912,4]{1,2,0:T(4,128)(2,1)}), bf16[64,6912,4]{1,2,0:T(4,128)(2,1)S(1)}, u32[]{:S(2)}, u32[]{:S(2)}) async-start(bf16[64,6912,4]{1,2,0:T(4,128)(2,1)} %stack.4), calls=%async_computation | async-start | bytes 7077888 | tf_op jit(solution)/shard_map/all_to_all | solution.py:12
  23.8 4.2 %collective-permute-start = (bf16[1,8,48,256]{3,2,1,0:T(8,128)(2,1)}, bf16[1,8,48,256]{3,2,1,0:T(8,128)(2,1)}, u32[]{:S(2)}, u32[]{:S(2)}) collective-permute-start(bf16[1,8,48,256]{3,2,1,0:T(8,128)(2,1)} %param.5), channel_id=1, source_target_pairs={{0,8},{4,12},{8,16},{12,20},{16,24},{20,28},{24,32},{28,36},{32,40... | collective-permute-start | bytes 589832 | tf_op jit(solution)/shard_map/ppermute | solution.py:22
  28.0 5.6 %collective-permute-start.1 = (bf16[1,8,48,256]{3,2,1,0:T(8,128)(2,1)}, bf16[1,8,48,256]{3,2,1,0:T(8,128)(2,1)}, u32[]{:S(2)}, u32[]{:S(2)}) collective-permute-start(bf16[1,8,48,256]{3,2,1,0:T(8,128)(2,1)} %param.5), channel_id=1, source_target_pairs={{0,4},{4,8},{8,12},{12,16},{16,20},{20,24},{24,28},{28,32},{32,36}... | collective-permute-start | bytes 589832 | tf_op jit(solution)/shard_map/ppermute | solution.py:22
  33.6 75.2 %collective-permute-done = bf16[1,8,48,256]{3,2,1,0:T(8,128)(2,1)} collective-permute-done((bf16[1,8,48,256]{3,2,1,0:T(8,128)(2,1)}, bf16[1,8,48,256]{3,2,1,0:T(8,128)(2,1)}, u32[]{:S(2)}, u32[]{:S(2)}) %collective-permute-start) | collective-permute-done | bytes 196640 | tf_op jit(solution)/shard_map/ppermute | solution.py:22
  111.6 1.9 collective-permute-start.2
  113.5 3.6 %collective-permute-start.3 = (bf16[3,1,48,256]{3,2,1,0:T(8,128)(2,1)S(1)}, bf16[3,1,48,256]{3,2,1,0:T(8,128)(2,1)S(1)}, u32[]{:S(2)}, u32[]{:S(2)}) collective-permute-start(bf16[3,1,48,256]{3,2,1,0:T(8,128)(2,1)S(1)} %get-tuple-element.113), channel_id=1, source_target_pairs={{1,0},{2,1},{3,2},{5,4},{6,5},{7,6},{9,8},{10,9},{11,10},{13,12},{... | collective-permute-start | bytes 221192 | tf_op jit(solution)/shard_map/ppermute | solution.py:33
  120.6 1.8 fusion.84
  122.5 3.6 stack.5
  126.1 17.4 %all-to-all-start.1 = ((bf16[64,6912,4]{1,2,0:T(4,128)(2,1)}), bf16[64,6912,4]{1,2,0:T(4,128)(2,1)S(1)}, u32[]{:S(2)}, u32[]{:S(2)}) async-start(bf16[64,6912,4]{1,2,0:T(4,128)(2,1)} %stack.5), calls=%async_computation.1 | async-start | bytes 7077888 | tf_op jit(solution)/shard_map/all_to_all | solution.py:12
  143.5 2.5 fusion.82
  146.1 1.6 slice.544
  149.2 1.6 slice.550
  150.8 1.6 slice.553
  152.4 1.6 slice.558
  155.6 1.6 slice.561
  157.2 3.9 %fusion.81 = (bf16[256,64,4]{0,2,1:T(4,128)(2,1)}, bf16[256,64,4]{0,2,1:T(4,128)(2,1)}, bf16[256,64,4]{0,2,1:T(4,128)(2,1)}, bf16[256,64,4]{0,2,1:T(4,128)(2,1)}...) fusion(bf16[6912,64,4]{0,2,1:T(4,128)(2,1)} %bitcast.349), kind=kLoop, calls=%fused_computation.142 | loop fusion | bytes 4980736 | tf_op jit(solution)/shard_map/slice | solution.py:88
  161.1 1.6 slice.567
  162.7 1.6 slice.564
  165.9 1.6 slice.576
  169.1 1.6 slice.579
  173.9 1.6 slice.587
  175.5 1.6 slice.593
  177.1 1.6 slice.590
  181.8 1.6 slice.599
  183.4 1.6 slice.605
  185.0 1.6 slice.607
  189.8 1.6 slice.619
  207.0 4.2 %collective-permute-start.4 = (bf16[1,8,48,256]{3,2,1,0:T(8,128)(2,1)}, bf16[1,8,48,256]{3,2,1,0:T(8,128)(2,1)}, u32[]{:S(2)}, u32[]{:S(2)}) collective-permute-start(bf16[1,8,48,256]{3,2,1,0:T(8,128)(2,1)} %bitcast.28), channel_id=1, source_target_pairs={{0,8},{4,12},{8,16},{12,20},{16,24},{20,28},{24,32},{28,36},{32,40... | collective-permute-start | bytes 589832 | tf_op jit(solution)/shard_map/ppermute | solution.py:22
  211.1 5.6 %collective-permute-start.5 = (bf16[1,8,48,256]{3,2,1,0:T(8,128)(2,1)}, bf16[1,8,48,256]{3,2,1,0:T(8,128)(2,1)}, u32[]{:S(2)}, u32[]{:S(2)}) collective-permute-start(bf16[1,8,48,256]{3,2,1,0:T(8,128)(2,1)} %bitcast.28), channel_id=1, source_target_pairs={{0,4},{4,8},{8,12},{12,16},{16,20},{20,24},{24,28},{28,32},{32,36}... | collective-permute-start | bytes 589832 | tf_op jit(solution)/shard_map/ppermute | solution.py:22
  216.7 24.6 %all-to-all-done.1 = bf16[64,6912,4]{1,2,0:T(4,128)(2,1)S(1)} async-done(((bf16[64,6912,4]{1,2,0:T(4,128)(2,1)}), bf16[64,6912,4]{1,2,0:T(4,128)(2,1)S(1)}, u32[]{:S(2)}, u32[]{:S(2)}) %all-to-all-start.1) | async-done | bytes 3538976 | tf_op jit(solution)/shard_map/all_to_all | solution.py:12
  241.3 2.1 fusion.79
  244.9 3.0 collective-permute-start.7
  259.5 2.0 collective-permute-start.6
  262.7 2.7 collective-permute-done.6
  266.6 1.6 select_maximum_fusion
  278.7 7.4 %all_gather.9 = bf16[384,1024]{1,0:T(8,128)(2,1)S(1)} all-gather(bf16[96,1024]{1,0:T(8,128)(2,1)S(1)} %reshape.138), channel_id=1, replica_groups=mesh['wide'=64,'narrow'=4] {'narrow'}, dimensions={0}, use_global_device_ids=true | all-gather | bytes 983040 | tf_op jit(solution)/shard_map/all_gather | solution.py:114
  286.1 5.5 %copy.31 = bf16[5,8,64,1024]{3,2,1,0:T(8,128)(2,1)S(1)} copy(bf16[5,8,64,1024]{3,1,2,0:T(8,128)(2,1)} %bitcast.350) | data formatting | bytes 10485760
  291.6 2.6 fusion.12
  296.7 4.2 %fusion.86 = (bf16[560]{0:T(1024)(128)(2,1)S(1)}, bf16[384,560]{0,1:T(8,128)(2,1)S(1)}) fusion(bf16[384,2240]{0,1:T(8,128)(2,1)} %convert_element_type.63, bf16[3,2240,560]{1,2,0:T(8,128)(2,1)} %param.9), kind=kOutput, calls=%fused_computation.147 | convolution fusion | flops 964668864 | bytes 4732000 | tf_op jit(solution)/shard_map/dot_general | solution.py:119
  300.9 3.2 fusion.22
  305.7 10.3 %all-to-all-start.2 = ((bf16[64,1,989]{2,1,0:T(2,128)(2,1)}), bf16[64,1,989]{2,1,0:T(2,128)(2,1)S(1)}, u32[]{:S(2)}, u32[]{:S(2)}) async-start(bf16[64,1,989]{2,1,0:T(2,128)(2,1)} %convert_element_type.72), calls=%async_computation.2 | async-start | bytes 524288 | tf_op jit(solution)/shard_map/all_to_all | solution.py:56
  316.0 3.5 fusion.49
  319.5 10.6 %all-to-all-done.2 = bf16[64,1,989]{2,1,0:T(2,128)(2,1)S(1)} async-done(((bf16[64,1,989]{2,1,0:T(2,128)(2,1)}), bf16[64,1,989]{2,1,0:T(2,128)(2,1)S(1)}, u32[]{:S(2)}, u32[]{:S(2)}) %all-to-all-start.2) | async-done | bytes 126624 | tf_op jit(solution)/shard_map/all_to_all | solution.py:56
  331.2 6.2 %all-to-all-start.3 = ((bf16[64,1,989]{2,1,0:T(2,128)(2,1)}), bf16[64,1,989]{2,1,0:T(2,128)(2,1)S(1)}, u32[]{:S(2)}, u32[]{:S(2)}) async-start(bf16[64,1,989]{2,1,0:T(2,128)(2,1)} %copy.24), calls=%async_computation.3 | async-start | bytes 524288 | tf_op jit(solution)/shard_map/all_to_all | solution.py:158
  337.5 1.8 select_reduce_fusion
  339.3 11.7 %all-to-all-done.3 = bf16[64,1,989]{2,1,0:T(2,128)(2,1)S(1)} async-done(((bf16[64,1,989]{2,1,0:T(2,128)(2,1)}), bf16[64,1,989]{2,1,0:T(2,128)(2,1)S(1)}, u32[]{:S(2)}, u32[]{:S(2)}) %all-to-all-start.3) | async-done | bytes 126624 | tf_op jit(solution)/shard_map/all_to_all | solution.py:158
  352.8 2.6 fusion.25
  (271 shorter events, 69.7 us)
Async XLA Ops:
  10.1 112.4 %all-to-all-start = ((bf16[64,6912,4]{1,2,0:T(4,128)(2,1)}), bf16[64,6912,4]{1,2,0:T(4,128)(2,1)S(1)}, u32[]{:S(2)}, u32[]{:S(2)}) async-start(bf16[64,6912,4]{1,2,0:T(4,128)(2,1)} %stack.4), calls=%async_computation | async-start | bytes 7077888 | tf_op jit(solution)/shard_map/all_to_all | solution.py:12
  23.8 262.3 %all-gather.3.cloned.1.call-start = ((), (), s32[]{:S(2)}) async-start(), calls=%async_computation.4 | async-start | bytes 5324800 | tf_op jit(solution)/shard_map/all_gather | solution.py:48
  23.8 84.9 %collective-permute-start = (bf16[1,8,48,256]{3,2,1,0:T(8,128)(2,1)}, bf16[1,8,48,256]{3,2,1,0:T(8,128)(2,1)}, u32[]{:S(2)}, u32[]{:S(2)}) collective-permute-start(bf16[1,8,48,256]{3,2,1,0:T(8,128)(2,1)} %param.5), channel_id=1, source_target_pairs={{0,8},{4,12},{8,16},{12,20},{16,24},{20,28},{24,32},{28,36},{32,40... | collective-permute-start | bytes 589832 | tf_op jit(solution)/shard_map/ppermute | solution.py:22
  28.0 81.7 %collective-permute-start.1 = (bf16[1,8,48,256]{3,2,1,0:T(8,128)(2,1)}, bf16[1,8,48,256]{3,2,1,0:T(8,128)(2,1)}, u32[]{:S(2)}, u32[]{:S(2)}) collective-permute-start(bf16[1,8,48,256]{3,2,1,0:T(8,128)(2,1)} %param.5), channel_id=1, source_target_pairs={{0,4},{4,8},{8,12},{12,16},{16,20},{20,24},{24,28},{28,32},{32,36}... | collective-permute-start | bytes 589832 | tf_op jit(solution)/shard_map/ppermute | solution.py:22
  111.6 6.3 %collective-permute-start.2 = (bf16[3,1,48,256]{3,2,1,0:T(8,128)(2,1)S(1)}, bf16[3,1,48,256]{3,2,1,0:T(8,128)(2,1)S(1)}, u32[]{:S(2)}, u32[]{:S(2)}) collective-permute-start(bf16[3,1,48,256]{3,2,1,0:T(8,128)(2,1)S(1)} %get-tuple-element.112), channel_id=1, source_target_pairs={{0,1},{1,2},{2,3},{4,5},{5,6},{6,7},{8,9},{9,10},{10,11},{12,13},{... | collective-permute-start | bytes 221192 | tf_op jit(solution)/shard_map/ppermute | solution.py:30
  113.5 5.6 %collective-permute-start.3 = (bf16[3,1,48,256]{3,2,1,0:T(8,128)(2,1)S(1)}, bf16[3,1,48,256]{3,2,1,0:T(8,128)(2,1)S(1)}, u32[]{:S(2)}, u32[]{:S(2)}) collective-permute-start(bf16[3,1,48,256]{3,2,1,0:T(8,128)(2,1)S(1)} %get-tuple-element.113), channel_id=1, source_target_pairs={{1,0},{2,1},{3,2},{5,4},{6,5},{7,6},{9,8},{10,9},{11,10},{13,12},{... | collective-permute-start | bytes 221192 | tf_op jit(solution)/shard_map/ppermute | solution.py:33
  122.5 3.6 copy-start
  126.1 115.2 %all-to-all-start.1 = ((bf16[64,6912,4]{1,2,0:T(4,128)(2,1)}), bf16[64,6912,4]{1,2,0:T(4,128)(2,1)S(1)}, u32[]{:S(2)}, u32[]{:S(2)}) async-start(bf16[64,6912,4]{1,2,0:T(4,128)(2,1)} %stack.5), calls=%async_computation.1 | async-start | bytes 7077888 | tf_op jit(solution)/shard_map/all_to_all | solution.py:12
  193.0 4.0 %copy-start.8 = (bf16[1,8,48,256]{3,2,1,0:T(8,128)(2,1)S(1)}, bf16[1,8,48,256]{3,2,1,0:T(8,128)(2,1)}, u32[]{:S(2)}) copy-start(bf16[1,8,48,256]{3,2,1,0:T(8,128)(2,1)} %get-tuple-element.86) | copy-start | bytes 589828
  193.0 4.0 %copy-start.62 = (bf16[256,256]{0,1:T(8,128)(2,1)S(1)}, bf16[256,256]{0,1:T(8,128)(2,1)}, u32[]{:S(2)}) copy-start(bf16[256,256]{0,1:T(8,128)(2,1)} %slice.576) | copy-start | bytes 393220
  193.0 4.2 %copy-start.7 = (bf16[1,8,48,256]{3,2,1,0:T(8,128)(2,1)S(1)}, bf16[1,8,48,256]{3,2,1,0:T(8,128)(2,1)}, u32[]{:S(2)}) copy-start(bf16[1,8,48,256]{3,2,1,0:T(8,128)(2,1)} %get-tuple-element.84) | copy-start | bytes 589828
  193.0 4.2 %copy-start.63 = (bf16[256,256]{0,1:T(8,128)(2,1)S(1)}, bf16[256,256]{0,1:T(8,128)(2,1)}, u32[]{:S(2)}) copy-start(bf16[256,256]{0,1:T(8,128)(2,1)} %slice.584) | copy-start | bytes 393220
  193.0 4.5 %copy-start.6 = (bf16[1,8,48,256]{3,2,1,0:T(8,128)(2,1)S(1)}, bf16[1,8,48,256]{3,2,1,0:T(8,128)(2,1)}, u32[]{:S(2)}) copy-start(bf16[1,8,48,256]{3,2,1,0:T(8,128)(2,1)} %get-tuple-element.82) | copy-start | bytes 589828
  193.0 4.5 %copy-start.64 = (bf16[256,256]{0,1:T(8,128)(2,1)S(1)}, bf16[256,256]{0,1:T(8,128)(2,1)}, u32[]{:S(2)}) copy-start(bf16[256,256]{0,1:T(8,128)(2,1)} %slice.593) | copy-start | bytes 393220
  194.3 3.4 copy-start.5
  194.3 3.4 copy-start.65
  195.6 2.4 copy-start.23
  195.6 2.4 copy-start.31
  198.3 1.9 copy-start.16
  198.3 1.9 copy-start.24
  198.6 1.9 copy-start.22
  198.6 1.9 copy-start.41
  199.0 1.8 copy-start.39
  201.2 1.8 copy-start.13
  201.2 1.8 copy-start.35
  201.8 1.8 copy-start.12
  207.0 36.3 %collective-permute-start.4 = (bf16[1,8,48,256]{3,2,1,0:T(8,128)(2,1)}, bf16[1,8,48,256]{3,2,1,0:T(8,128)(2,1)}, u32[]{:S(2)}, u32[]{:S(2)}) collective-permute-start(bf16[1,8,48,256]{3,2,1,0:T(8,128)(2,1)} %bitcast.28), channel_id=1, source_target_pairs={{0,8},{4,12},{8,16},{12,20},{16,24},{20,28},{24,32},{28,36},{32,40... | collective-permute-start | bytes 589832 | tf_op jit(solution)/shard_map/ppermute | solution.py:22
  211.1 32.2 %collective-permute-start.5 = (bf16[1,8,48,256]{3,2,1,0:T(8,128)(2,1)}, bf16[1,8,48,256]{3,2,1,0:T(8,128)(2,1)}, u32[]{:S(2)}, u32[]{:S(2)}) collective-permute-start(bf16[1,8,48,256]{3,2,1,0:T(8,128)(2,1)} %bitcast.28), channel_id=1, source_target_pairs={{0,4},{4,8},{8,12},{12,16},{16,20},{20,24},{24,28},{28,32},{32,36}... | collective-permute-start | bytes 589832 | tf_op jit(solution)/shard_map/ppermute | solution.py:22
  244.9 16.7 %collective-permute-start.7 = (bf16[3,1,48,256]{3,2,1,0:T(8,128)(2,1)}, bf16[3,1,48,256]{3,2,1,0:T(8,128)(2,1)}, u32[]{:S(2)}, u32[]{:S(2)}) collective-permute-start(bf16[3,1,48,256]{3,2,1,0:T(8,128)(2,1)} %get-tuple-element.108), channel_id=1, source_target_pairs={{1,0},{2,1},{3,2},{5,4},{6,5},{7,6},{9,8},{10,9},{11,10},{13,12},{... | collective-permute-start | bytes 221192 | tf_op jit(solution)/shard_map/ppermute | solution.py:33
  249.0 8.0 %copy-start.59 = (bf16[256,64,4]{0,2,1:T(4,128)(2,1)S(1)}, bf16[256,64,4]{0,2,1:T(4,128)(2,1)}, u32[]{:S(2)}) copy-start(bf16[256,64,4]{0,2,1:T(4,128)(2,1)} %get-tuple-element.24) | copy-start | bytes 393220
  249.0 9.0 %copy-start.58 = (bf16[256,64,4]{0,2,1:T(4,128)(2,1)S(1)}, bf16[256,64,4]{0,2,1:T(4,128)(2,1)}, u32[]{:S(2)}) copy-start(bf16[256,64,4]{0,2,1:T(4,128)(2,1)} %get-tuple-element.20) | copy-start | bytes 393220
  249.0 9.1 %copy-start.57 = (bf16[256,64,4]{0,2,1:T(4,128)(2,1)S(1)}, bf16[256,64,4]{0,2,1:T(4,128)(2,1)}, u32[]{:S(2)}) copy-start(bf16[256,64,4]{0,2,1:T(4,128)(2,1)} %get-tuple-element.21) | copy-start | bytes 393220
  249.0 9.1 %copy-start.56 = (bf16[256,64,4]{0,2,1:T(4,128)(2,1)S(1)}, bf16[256,64,4]{0,2,1:T(4,128)(2,1)}, u32[]{:S(2)}) copy-start(bf16[256,64,4]{0,2,1:T(4,128)(2,1)} %get-tuple-element.19) | copy-start | bytes 393220
  249.0 9.2 %copy-start.55 = (bf16[256,64,4]{0,2,1:T(4,128)(2,1)S(1)}, bf16[256,64,4]{0,2,1:T(4,128)(2,1)}, u32[]{:S(2)}) copy-start(bf16[256,64,4]{0,2,1:T(4,128)(2,1)} %get-tuple-element.17) | copy-start | bytes 393220
  250.1 8.8 %copy-start.54 = (bf16[256,64,4]{0,2,1:T(4,128)(2,1)S(1)}, bf16[256,64,4]{0,2,1:T(4,128)(2,1)}, u32[]{:S(2)}) copy-start(bf16[256,64,4]{0,2,1:T(4,128)(2,1)} %get-tuple-element.18) | copy-start | bytes 393220
  251.0 7.9 %copy-start.53 = (bf16[256,64,4]{0,2,1:T(4,128)(2,1)S(1)}, bf16[256,64,4]{0,2,1:T(4,128)(2,1)}, u32[]{:S(2)}) copy-start(bf16[256,64,4]{0,2,1:T(4,128)(2,1)} %get-tuple-element.16) | copy-start | bytes 393220
  252.0 7.0 %copy-start.52 = (bf16[256,64,4]{0,2,1:T(4,128)(2,1)S(1)}, bf16[256,64,4]{0,2,1:T(4,128)(2,1)}, u32[]{:S(2)}) copy-start(bf16[256,64,4]{0,2,1:T(4,128)(2,1)} %get-tuple-element.14) | copy-start | bytes 393220
  253.0 6.0 %copy-start.51 = (bf16[256,64,4]{0,2,1:T(4,128)(2,1)S(1)}, bf16[256,64,4]{0,2,1:T(4,128)(2,1)}, u32[]{:S(2)}) copy-start(bf16[256,64,4]{0,2,1:T(4,128)(2,1)} %get-tuple-element.15) | copy-start | bytes 393220
  254.0 5.1 %copy-start.50 = (bf16[256,64,4]{0,2,1:T(4,128)(2,1)S(1)}, bf16[256,64,4]{0,2,1:T(4,128)(2,1)}, u32[]{:S(2)}) copy-start(bf16[256,64,4]{0,2,1:T(4,128)(2,1)} %get-tuple-element.13) | copy-start | bytes 393220
  255.0 4.1 %copy-start.49 = (bf16[256,64,4]{0,2,1:T(4,128)(2,1)S(1)}, bf16[256,64,4]{0,2,1:T(4,128)(2,1)}, u32[]{:S(2)}) copy-start(bf16[256,64,4]{0,2,1:T(4,128)(2,1)} %get-tuple-element.11) | copy-start | bytes 393220
  256.0 3.2 copy-start.48
  257.0 2.3 copy-start.47
  257.0 2.3 copy-start.46
  259.5 5.9 %collective-permute-start.6 = (bf16[3,1,48,256]{3,2,1,0:T(8,128)(2,1)}, bf16[3,1,48,256]{3,2,1,0:T(8,128)(2,1)S(1)}, u32[]{:S(2)}, u32[]{:S(2)}) collective-permute-start(bf16[3,1,48,256]{3,2,1,0:T(8,128)(2,1)} %get-tuple-element.107), channel_id=1, source_target_pairs={{0,1},{1,2},{2,3},{4,5},{5,6},{6,7},{8,9},{9,10},{10,11},{12,13},{... | collective-permute-start | bytes 221192 | tf_op jit(solution)/shard_map/ppermute | solution.py:30
  296.7 4.2 %copy-start.3 = (bf16[384,2240]{0,1:T(8,128)(2,1)S(1)}, bf16[384,2240]{0,1:T(8,128)(2,1)}, u32[]{:S(2)}) copy-start(bf16[384,2240]{0,1:T(8,128)(2,1)} %convert_element_type.63) | copy-start | bytes 5160964
  305.7 24.5 %all-to-all-start.2 = ((bf16[64,1,989]{2,1,0:T(2,128)(2,1)}), bf16[64,1,989]{2,1,0:T(2,128)(2,1)S(1)}, u32[]{:S(2)}, u32[]{:S(2)}) async-start(bf16[64,1,989]{2,1,0:T(2,128)(2,1)} %convert_element_type.72), calls=%async_computation.2 | async-start | bytes 524288 | tf_op jit(solution)/shard_map/all_to_all | solution.py:56
  316.0 21.4 %copy-start.67 = (pred[384,384]{0,1:T(8,128)(4,1)S(1)}, pred[384,384]{0,1:T(8,128)(4,1)}, u32[]{:S(2)}) copy-start(pred[384,384]{0,1:T(8,128)(4,1)} %iota_compare_fusion.2) | copy-start | bytes 442372
  331.2 19.7 %all-to-all-start.3 = ((bf16[64,1,989]{2,1,0:T(2,128)(2,1)}), bf16[64,1,989]{2,1,0:T(2,128)(2,1)S(1)}, u32[]{:S(2)}, u32[]{:S(2)}) async-start(bf16[64,1,989]{2,1,0:T(2,128)(2,1)} %copy.24), calls=%async_computation.3 | async-start | bytes 524288 | tf_op jit(solution)/shard_map/all_to_all | solution.py:158
  (34 other events, 39.5 us)
Sparse Core Ops, SparseCore 0:
  33.7 174.2 all-gather.2
